TPU v7x, 32 devices: a whole 2x2x4 slice. The times are simulated.
32 devices in a mesh: groups: 2 (over x), sect: 8 (over z, y), head: 2 (over core).
Axes of the slice: x: 2, y: 2, z: 4, core: 2. Of those that a mesh axis runs over, the one named last changes fastest.
Arguments:
- queries: bfloat16 [2048, 8192], P(('groups', 'sect'), 'head'), parts along dimension 0, may hold values from -200 to 200
- packed_key_rows: bfloat16 [2048, 512], P(('groups', 'sect'), 'head'), parts along dimension 0, may hold values from -7 to 7
- values: bfloat16 [2048, 512], P(('groups', 'sect'), 'head'), parts along dimension 0, may hold values from -12 to 12
- segments: int32 [2048], P('groups'), parts along dimension 0, may hold values from 0 to 7, never falling along the last dimension, each value on 1 to 512 neighbouring positions
- proj_weight: bfloat16 [8192, 2048], P('head', 'sect'), may hold values from -0.0625 to 0.0625
- residual: bfloat16 [2048, 2048], P(('groups', 'sect', 'head')), parts along dimension 0, may hold values from -2 to 2
- norm_gain: bfloat16 [2048], replicated, may hold values from 0.5 to 1.5
- expert_ids: int32 [2048, 8], P(('groups', 'sect', 'head')), parts along dimension 0, may hold values from 0 to 15, all different within a row; in each aligned block of 64 rows (0 to 63, 64 to 127, ...) at most 48 rows name the same one
- route_weights: float32 [2048, 8], P(('groups', 'sect', 'head')), parts along dimension 0, may hold values from 0.05 to 1
- gate_weight: bfloat16 [16, 2048, 768], P(('sect', 'head')), may hold values from -0.125 to 0.125
- up_weight: bfloat16 [16, 2048, 768], P(('sect', 'head')), may hold values from -0.125 to 0.125
- down_weight: bfloat16 [16, 768, 2048], P(('sect', 'head')), may hold values from -0.21875 to 0.21875
Outputs:
- hidden_mid: bfloat16 [2048, 2048], P(('groups', 'sect', 'head')), parts along dimension 0
- expert_mix: bfloat16 [2048, 2048], P(('groups', 'sect', 'head')), parts along dimension 0
There are 2 independent parts, one for each index of `groups`. A program takes and returns all parts, laid end to end along the dimension named above; an argument that names none is the same for every part. Nothing has to cross between parts.
Inputs may be any that keep to these rules, and one draw needn't show every extreme that they name: `segments`: ids never fall along the rows; each of the 8 prompts has 1 to 512 rows, and one has exactly that many. `expert_ids`: each row names 8 different experts. Within the rows of one device (aligned blocks of 64 rows) no expert is named by more than 48 rows.
All inputs are finite; a program needn't handle non-finite values.
Results may differ from a plain program's by a relative error of at most 0.02.
Values may be sent and summed in bfloat16 or wider, within the bound.
A program may use at most 256 MiB of HBM per device.

v0:
```python
import math

import jax
import jax.numpy as jnp
from jax import lax
from jax.sharding import PartitionSpec as P

HEAD_WIDTH = 128


negative_large = -1e30
norm_eps = 1e-06


def attend(query_groups, packed_key_rows, values, segments, head_size):
    kv_heads = packed_key_rows.shape[1] // head_size
    score_scale = 1.0 / math.sqrt(head_size)
    prepared = []
    initial_state = []
    for query_rows, query_pos in query_groups:
        query_count = query_rows.shape[0]
        query_group_width = query_rows.shape[1] // head_size // kv_heads
        query_tensor_four = query_rows.reshape(query_count, kv_heads, query_group_width, head_size)
        query_seg = jnp.take(segments, query_pos)
        seg_start = jnp.sum((segments[None, :] < query_seg[:, None]).astype(jnp.int32), axis=1)
        prepared.append(
            (query_tensor_four, query_pos, query_seg, jnp.min(seg_start), jnp.max(query_pos))
        )
        initial_state.append(
            (
                jnp.full((query_count, kv_heads, query_group_width), negative_large, jnp.float32),
                jnp.zeros((query_count, kv_heads, query_group_width), jnp.float32),
                jnp.zeros((query_count, kv_heads, query_group_width, head_size), jnp.float32),
            )
        )
    running = tuple(initial_state)
    first_row = jnp.int32(0)
    key_piece = lax.all_gather(packed_key_rows, "sect", axis=0, tiled=True)
    value_piece = lax.all_gather(values, "sect", axis=0, tiled=True)
    piece_len = key_piece.shape[0]
    key_tensor_three = key_piece.reshape(piece_len, kv_heads, head_size)
    value_tensor_three = value_piece.reshape(piece_len, kv_heads, head_size)
    key_pos = jnp.arange(piece_len, dtype=jnp.int32)
    updated = []
    for state, setup in zip(running, prepared):
        query_tensor_four, query_pos, query_seg, lowest, highest = setup
        needed = jnp.logical_and(first_row <= highest, first_row + piece_len - 1 >= lowest)

        def compute(
            current, query_tensor_four=query_tensor_four, query_pos=query_pos, query_seg=query_seg
        ):
            run_max, run_sum, run_acc = current
            scores = (
                jnp.einsum(
                    "rkgd,pkd->rkgp",
                    query_tensor_four,
                    key_tensor_three,
                    preferred_element_type=jnp.float32,
                )
                * score_scale
            )
            allowed = jnp.logical_and(
                segments[None, :] == query_seg[:, None], key_pos[None, :] <= query_pos[:, None]
            )
            allowed = allowed[:, None, None, :]
            block_max = jnp.max(jnp.where(allowed, scores, negative_large), axis=-1)
            new_max = jnp.maximum(run_max, block_max)
            weights = jnp.where(allowed, jnp.exp(scores - new_max[..., None]), 0.0).astype(
                jnp.bfloat16
            )
            new_sum = jnp.sum(weights.astype(jnp.float32), axis=-1)
            new_acc = jnp.einsum(
                "rkgp,pkd->rkgd", weights, value_tensor_three, preferred_element_type=jnp.float32
            )
            return (new_max, new_sum, new_acc)

        updated.append(lax.cond(needed, compute, lambda kept: kept, state))
    final_state = tuple(updated)
    results = []
    for run_max, run_sum, run_acc in final_state:
        attended = run_acc / run_sum[..., None]
        results.append(attended.reshape(attended.shape[0], -1).astype(jnp.bfloat16))
    return results


def shards(
    queries,
    packed_key_rows,
    values,
    segments,
    proj_weight,
    residual,
    norm_gain,
    expert_ids,
    route_weights,
    gate_weight,
    up_weight,
    down_weight,
):
    row_count = queries.shape[0]
    sect_count = lax.axis_size("sect")
    head_count = lax.axis_size("head")
    sect_pos = lax.axis_index("sect")
    local_pos = jnp.arange(row_count, dtype=jnp.int32)
    own_pos = sect_pos * row_count + local_pos
    attended = attend([(queries, own_pos)], packed_key_rows, values, segments, HEAD_WIDTH)[0]
    partial_value = jnp.dot(
        attended,
        lax.all_gather(proj_weight, "sect", axis=1, tiled=True),
        preferred_element_type=jnp.float32,
    )
    projected = lax.psum_scatter(
        partial_value.astype(jnp.bfloat16), "head", scatter_dimension=0, tiled=True
    ).astype(jnp.float32)
    hidden_mid = (residual.astype(jnp.float32) + projected).astype(jnp.bfloat16)
    mid_float = lax.optimization_barrier(hidden_mid).astype(jnp.float32)
    inverse = lax.rsqrt(jnp.mean(mid_float * mid_float, axis=1, keepdims=True) + norm_eps)
    normed = (mid_float * inverse * norm_gain.astype(jnp.float32)[None, :]).astype(jnp.bfloat16)
    moe_rows = residual.shape[0]
    top_count = expert_ids.shape[1]
    experts = sect_count * head_count
    capacity = max(2, 3 * moe_rows * top_count // (2 * experts))
    flat_ids = expert_ids.reshape(-1)
    onehot = (flat_ids[:, None] == jnp.arange(experts, dtype=jnp.int32)[None, :]).astype(jnp.int32)
    slot_rank = jnp.sum((jnp.cumsum(onehot, axis=0) - 1) * onehot, axis=1)
    slot_index = flat_ids * capacity + slot_rank
    sources = jnp.repeat(normed, top_count, axis=0)
    outgoing = (
        jnp.zeros((experts * capacity, normed.shape[1]), jnp.bfloat16).at[slot_index].set(sources)
    )
    parcels = outgoing.reshape(experts, capacity, -1)
    slot_rows = lax.all_to_all(parcels, ("sect", "head"), split_axis=0, concat_axis=0, tiled=True)
    flat_rows = slot_rows.reshape(-1, slot_rows.shape[-1])
    gate_act = jnp.dot(flat_rows, gate_weight[0], preferred_element_type=jnp.float32)
    up_act = jnp.dot(flat_rows, up_weight[0], preferred_element_type=jnp.float32)
    hidden = (jax.nn.silu(gate_act) * up_act).astype(jnp.bfloat16)
    result = jnp.dot(hidden, down_weight[0], preferred_element_type=jnp.float32).astype(
        jnp.bfloat16
    )
    processed = result.reshape(slot_rows.shape)
    returned_rows = lax.all_to_all(
        processed, ("sect", "head"), split_axis=0, concat_axis=0, tiled=True
    )
    returned_flat = returned_rows.reshape(experts * capacity, -1)
    gathered = returned_flat[slot_index].reshape(moe_rows, top_count, -1)
    route_share = route_weights / jnp.sum(route_weights, axis=1, keepdims=True)
    mixture = jnp.sum(route_share[:, :, None] * gathered.astype(jnp.float32), axis=1)
    return (hidden_mid, mixture.astype(jnp.bfloat16))


def solution(mesh):
    placed = (
        P(("groups", "sect"), "head"),
        P(("groups", "sect"), "head"),
        P(("groups", "sect"), "head"),
        P("groups"),
        P("head", "sect"),
        P(("groups", "sect", "head"), None),
        P(),
        P(("groups", "sect", "head"), None),
        P(("groups", "sect", "head"), None),
        P(("sect", "head"), None, None),
        P(("sect", "head"), None, None),
        P(("sect", "head"), None, None),
    )
    return jax.shard_map(
        shards,
        mesh=mesh,
        in_specs=placed,
        out_specs=(P(("groups", "sect", "head"), None), P(("groups", "sect", "head"), None)),
        check_vma=False,
    )
```

profile of v0, /device:TPU:17, one launch (start us, length us, event | category | flops | bytes accessed | tf_op | source)
XLA Modules:
  0.0 461.9 jit_solution(15963046055641040890)
XLA Ops:
  8.0 1.8 gather_fusion
  13.3 31.3 %all_gather.9 = bf16[1024,256]{1,0:T(8,128)(2,1)} all-gather(bf16[128,256]{1,0:T(8,128)(2,1)} %param.15), channel_id=1, replica_groups=mesh['groups'=2,'sect'=8,'head'=2] {'sect'}, dimensions={0}, use_global_device_ids=true | all-gather | bytes 589824 | tf_op jit(solution)/shard_map/all_gather | solution.py:38
  44.6 33.0 %all_gather.10 = bf16[1024,256]{1,0:T(8,128)(2,1)} all-gather(bf16[128,256]{1,0:T(8,128)(2,1)S(1)} %copy-done.4), channel_id=1, replica_groups=mesh['groups'=2,'sect'=8,'head'=2] {'sect'}, dimensions={0}, use_global_device_ids=true | all-gather | bytes 589824 | tf_op jit(solution)/shard_map/all_gather | solution.py:39
  77.6 40.8 %conditional.1 = (f32[128,2,16]{0,2,1:T(8,128)S(1)}, f32[128,2,16,128]{0,3,2,1:T(8,128)}) conditional(s32[]{:T(128)} %convert_element_type.61, () %tuple.16, (s32[1024]{0:T(1024)S(1)}, s32[128]{0:T(128)S(1)}, s32[128]{0:T(128)S(1)}, s32[128]{0:T(128)S(1)}, s32[1024]{0:T(1024)S(1)}, /*index=5*/s32[128]{0:T(128)S(1)}, bf16[1024,256]{1,0:T(8,128)(2,1)}, ...), branch_computations={%region_3.4_spmd, %region_4.0_spmd} | conditional | flops 2202399232 | bytes 63548432 | solution.py:77
  78.0 2.4 copy.61
  80.5 2.0 reshape.167
  82.4 9.8 %fusion = (f32[128,2,16]{0,2,1:T(8,128)S(1)}, f32[2,1024,128,16]{2,1,3,0:T(8,128)}) fusion(pred[128,1024]{0,1:T(8,128)(4,1)S(1)} %compare_and_fusion, bf16[128,2,16,128]{3,2,1,0:T(8,128)(2,1)} %bitcast.70, bf16[1024,2,128,1]{2,1,0,3:T(2,128)(2,1)} %bitcast.74), kind=kOutput, calls=%fused_computation.5 | convolution fusion | flops 1086320640 | bytes 18497536 | tf_op jit(solution)/shard_map/cond/branch_1_fun/rkgd,pkd->rkgp/dot_general | solution.py:54
  92.2 9.2 %convert_reduce_fusion = f32[128,2,16]{0,2,1:T(8,128)S(1)} fusion(f32[128,2,16]{0,2,1:T(8,128)S(1)} %broadcast_maximum_fusion, f32[2,1024,128,16]{2,1,3,0:T(8,128)} %get-tuple-element.49, pred[128,1024]{0,1:T(8,128)(4,1)S(1)} %compare_and_fusion), kind=kLoop, calls=%fused_computation.9 | loop fusion | flops 25161728 | bytes 16941056 | tf_op jit(solution)/shard_map/cond/branch_1_fun/reduce_sum | solution.py:71
  101.4 2.0 reshape.169
  103.4 12.1 %convolution_bitcast_fusion = f32[128,2,16,128]{3,0,2,1:T(8,128)} fusion(bf16[1024,2,128,1]{2,1,0,3:T(2,128)(2,1)} %bitcast.76, f32[2,1024,128,16]{2,1,3,0:T(8,128)} %get-tuple-element.49, f32[128,2,16]{0,2,1:T(8,128)S(1)} %broadcast_maximum_fusion, pred[128,1024]{0,1:T(8,128)(4,1)S(1)} %compare_and_fusion), kind=kOutput, calls=%fused_computation.10 | convolution fusion | flops 1090519040 | bytes 19546112 | tf_op jit(solution)/shard_map/cond/branch_1_fun/rkgp,pkd->rkgd/dot_general | solution.py:72
  115.5 3.0 copy.60
  118.5 2.9 divide_convert_fusion
  121.4 128.4 %all-gather.2.cloned.1.call-done = bf16[4096,2048]{1,0:T(8,128)(2,1)} async-done(((bf16[4096,256]{1,0:T(8,128)(2,1)}), bf16[4096,2048]{1,0:T(8,128)(2,1)}) %all-gather.2.cloned.1.call-update) | async-done | bytes 16777232 | tf_op jit(solution)/shard_map/all_gather | solution.py:109
  249.8 9.3 %convolution_convert_fusion.1 = bf16[128,2048]{1,0:T(8,128)(2,1)} fusion(bf16[128,4096]{0,1:T(8,128)(2,1)} %bitcast.69, bf16[4096,2048]{1,0:T(8,128)(2,1)} %all-gather.2.cloned.1.call-done), kind=kOutput, calls=%fused_computation.28 | convolution fusion | flops 2147745792 | bytes 18350080 | tf_op jit(solution)/shard_map/dot_general | solution.py:107
  261.1 6.6 %reduce-scatter.2.cloned.1.call-done = bf16[64,2048]{1,0:T(8,128)(2,1)} async-done(((bf16[128,2048]{1,0:T(8,128)(2,1)}), bf16[64,2048]{1,0:T(8,128)(2,1)}) %reduce-scatter.2.cloned.1.call-update) | async-done | bytes 262160 | tf_op jit(solution)/shard_map/reduce_scatter | solution.py:112
  269.8 6.1 %scatter_custom_fusion = bf16[768,2048]{1,0:T(8,128)(2,1)} fusion(s32[512]{0:T(512)S(1)} %bitcast.77, bf16[]{:T(256)} %constant.60.clone.1, bf16[64,2048]{1,0:T(8,128)(2,1)} %fusion.27), kind=kCustom, calls=%fused_computation.30 | custom fusion | bytes 3407874 | tf_op jit(solution)/shard_map/scatter | solution.py:129
  275.9 75.4 %all_to_all.10 = bf16[16,48,2048]{2,1,0:T(8,128)(2,1)S(1)} all-to-all(bf16[16,48,2048]{2,1,0:T(8,128)(2,1)} %bitcast.68), channel_id=1, replica_groups=mesh['groups'=2,'sect'=8,'head'=2] {'sect','head'}, dimensions={0} | all-to-all | bytes 6291456 | tf_op jit(solution)/shard_map/all_to_all | solution.py:132
  351.3 1.7 copy-done.2
  353.0 4.0 fusion.13
  357.0 11.0 %convolution_convert_fusion = bf16[768,2048]{1,0:T(8,128)(2,1)} fusion(bf16[1,768,2048]{2,1,0:T(8,128)(2,1)S(1)} %copy-done, f32[768,768]{1,0:T(8,128)} %fusion.13, bf16[768,2048]{1,0:T(8,128)(2,1)} %bitcast.73, bf16[1,2048,768]{2,1,0:T(8,128)(2,1)} %param.23), kind=kOutput, calls=%fused_computation.22 | convolution fusion | flops 4836950016 | bytes 14942208 | tf_op jit(solution)/shard_map/dot_general | solution.py:137
  368.0 5.7 %all-to-all-start.1 = ((bf16[16,48,2048]{2,1,0:T(8,128)(2,1)}), bf16[16,48,2048]{2,1,0:T(8,128)(2,1)}, u32[]{:S(2)}, u32[]{:S(2)}) async-start(bf16[16,48,2048]{2,1,0:T(8,128)(2,1)} %bitcast.71), calls=%async_computation.2 | async-start | bytes 6291456 | tf_op jit(solution)/shard_map/all_to_all | solution.py:141
  373.8 69.5 %all-to-all-done.1 = bf16[16,48,2048]{2,1,0:T(8,128)(2,1)} async-done(((bf16[16,48,2048]{2,1,0:T(8,128)(2,1)}), bf16[16,48,2048]{2,1,0:T(8,128)(2,1)}, u32[]{:S(2)}, u32[]{:S(2)}) %all-to-all-start.1) | async-done | bytes 3145760 | tf_op jit(solution)/shard_map/all_to_all | solution.py:141
  443.3 7.6 %gather_fusion.1 = bf16[512,2048]{1,0:T(8,128)(2,1)} fusion(bf16[768,2048]{1,0:T(8,128)(2,1)} %bitcast.16, s32[1024]{0:T(1024)S(1)} %pad_clamp_fusion), kind=kCustom, calls=%fused_computation.1 | custom fusion | bytes 4196352 | tf_op jit(solution)/shard_map/gather | solution.py:145
  450.9 4.1 fusion.11
  (54 shorter events, 7.5 us)
Async XLA Ops:
  7.2 349.8 %copy-start = (bf16[1,768,2048]{2,1,0:T(8,128)(2,1)S(1)}, bf16[1,768,2048]{2,1,0:T(8,128)(2,1)}, u32[]{:S(2)}) copy-start(bf16[1,768,2048]{2,1,0:T(8,128)(2,1)} %param.25) | copy-start | bytes 9437188
  7.2 70.5 %copy-start.1 = (s32[1024]{0:T(1024)S(1)}, s32[1024]{0:T(1024)}, u32[]{:S(2)}) copy-start(s32[1024]{0:T(1024)} %param.17) | copy-start | bytes 12292
  7.2 37.4 %copy-start.4 = (bf16[128,256]{1,0:T(8,128)(2,1)S(1)}, bf16[128,256]{1,0:T(8,128)(2,1)}, u32[]{:S(2)}) copy-start(bf16[128,256]{1,0:T(8,128)(2,1)} %param.16) | copy-start | bytes 196612
  7.2 242.6 %all-gather.2.cloned.1.call-start = ((), (), s32[]{:S(2)}) async-start(), calls=%async_computation.3 | async-start | bytes 18874368 | tf_op jit(solution)/shard_map/all_gather | solution.py:109
  7.9 259.8 %reduce-scatter.2.cloned.1.call-start = ((), (), s32[]{:S(2)}) async-start(), calls=%async_computation.4 | async-start | bytes 786432 | tf_op jit(solution)/shard_map/reduce_scatter | solution.py:112
  249.8 9.3 %copy-start.5 = (s32[64,8]{0,1:T(8,128)S(1)}, s32[64,8]{0,1:T(8,128)}, u32[]{:S(2)}) copy-start(s32[64,8]{0,1:T(8,128)} %param.21) | copy-start | bytes 6148
  249.8 11.2 %copy-start.7 = (bf16[2048]{0:T(1024)(128)(2,1)S(1)}, bf16[2048]{0:T(1024)(128)(2,1)}, u32[]{:S(2)}) copy-start(bf16[2048]{0:T(1024)(128)(2,1)} %param.20) | copy-start | bytes 12292
  268.8 82.5 %copy-start.3 = (bf16[64,2048]{1,0:T(8,128)(2,1)}, bf16[64,2048]{1,0:T(8,128)(2,1)S(1)}, u32[]{:S(2)}) copy-start(bf16[64,2048]{1,0:T(8,128)(2,1)S(1)} %add_convert_fusion) | copy-start | bytes 786436
  275.9 77.1 %copy-start.8 = (bf16[1,2048,768]{2,1,0:T(8,128)(2,1)S(1)}, bf16[1,2048,768]{2,1,0:T(8,128)(2,1)}, u32[]{:S(2)}) copy-start(bf16[1,2048,768]{2,1,0:T(8,128)(2,1)} %param.24) | copy-start | bytes 9437188
  351.3 1.7 copy-start.2
  368.0 5.7 %copy-start.6 = (f32[64,8]{0,1:T(8,128)S(1)}, f32[64,8]{0,1:T(8,128)}, u32[]{:S(2)}) copy-start(f32[64,8]{0,1:T(8,128)} %param.22) | copy-start | bytes 6148
  368.0 75.3 %all-to-all-start.1 = ((bf16[16,48,2048]{2,1,0:T(8,128)(2,1)}), bf16[16,48,2048]{2,1,0:T(8,128)(2,1)}, u32[]{:S(2)}, u32[]{:S(2)}) async-start(bf16[16,48,2048]{2,1,0:T(8,128)(2,1)} %bitcast.71), calls=%async_computation.2 | async-start | bytes 6291456 | tf_op jit(solution)/shard_map/all_to_all | solution.py:141
Sparse Core Ops, SparseCore 0:
  10.1 239.6 all-gather.1
  259.2 8.4 reduce-scatter.1
where the time goes:
time: 463 us; the launch traced here: 462 us
  waiting for transfers between devices  205 us (44%)
  blocking collectives  140 us (30%)
  matrix products  46.1 us (10%)
  local copies, waits for them, and re-layouts  27.3 us (6%)
  other arithmetic  22.3 us (5%)
  between operations  15.5 us (3%)
  starting transfers between devices  5.76 us (1%)
    all_gather x1, waiting for transfers between devices, shards(): lax.all_gather(proj_weight, 'sect', axis=1, tiled=True)  128 us
    all_to_all x1, blocking collectives, shards(): lax.all_to_all(parcels, ('sect', 'head'), split_axis=0, concat_axis=0, ti...  75.4 us
    all_to_all x1, waiting for transfers between devices, shards(): lax.all_to_all(processed, ('sect', 'head'), split_axis=0, concat_axis=0,...  69.5 us
    all_gather x1, blocking collectives, attend(): value_piece = lax.all_gather(values, 'sect', axis=0, tiled=True)  33 us
    all_gather x1, blocking collectives, attend(): key_piece = lax.all_gather(packed_key_rows, 'sect', axis=0, tiled=True)  31.3 us
    dot_general x1, matrix products, compute(): jnp.einsum('rkgp,pkd->rkgd', weights, value_tensor_three, preferred_eleme...  12.1 us
    dot_general x1, matrix products, shards(): jnp.dot(hidden, down_weight[0], preferred_element_type=jnp.float32)  11 us
    dot_general x1, matrix products, compute(): jnp.einsum('rkgd,pkd->rkgp', query_tensor_four, key_tensor_three, preferr...  9.76 us
  transfers between devices with their start and end apart: 3, of which 3 were waited for; matrix products, arithmetic and copies ran while one was open for 11% of the time, Pallas kernels for 0%

commit v1 on v0

v1 whole, which is shorter than its diff:
```python
import functools
import math

import jax
import jax.numpy as jnp
from jax import lax
from jax.experimental import pallas as pl
from jax.experimental.pallas import tpu as pltpu
from jax.sharding import PartitionSpec as P

HEAD_WIDTH = 128
MASKED = -1e30
NORM_EPS = 1e-06
MESH = pl.DeviceIdType.MESH
VMEM_SPEC = pl.BlockSpec(memory_space=pltpu.VMEM)
ANY_SPEC = pl.BlockSpec(memory_space=pl.ANY)
DMA = pltpu.SemaphoreType.DMA


def greet(devices):
    barrier = pltpu.get_barrier_semaphore()
    for device in devices:
        pl.semaphore_signal(barrier, inc=1, device_id=device, device_id_type=MESH)
    pl.semaphore_wait(barrier, len(devices))


def remote(src, dst, send_sem, recv_sem, device):
    return pltpu.make_async_remote_copy(
        src_ref=src,
        dst_ref=dst,
        send_sem=send_sem,
        recv_sem=recv_sem,
        device_id=device,
        device_id_type=MESH,
    )


def attention_kernel(
    groups,
    sects,
    kv_heads,
    q_ref,
    kv_ref,
    seg_q_ref,
    seg_k_ref,
    w_ref,
    a_out,
    w_out,
    kv_all,
    att,
    bias,
    kz_send,
    kz_recv,
    ky_send,
    ky_recv,
    a_send,
    a_recv,
    w_send,
    w_recv,
    f_send,
    f_recv,
    local_sem,
):
    g = lax.axis_index("groups")
    s = lax.axis_index("sect")
    halves = sects // 2
    h = s // 2
    low = lax.rem(s, 2)
    rows = q_ref.shape[0]
    cols = q_ref.shape[1] // sects
    w_cols = w_ref.shape[1]
    w_rows = w_ref.shape[0] // sects
    part = w_rows // groups
    other_y = 2 * h + 1 - low
    sect_peers = [lax.rem(s + i, sects) for i in range(1, sects)]
    group_peers = [lax.rem(g + i, groups) for i in range(1, groups)]
    greet([{"sect": t} for t in sect_peers] + [{"groups": t} for t in group_peers])
    started = []

    def kv_cross(t):
        return remote(
            kv_ref if t is None else kv_all.at[2 * t + low],
            kv_all.at[s if t is None else 2 * t + low],
            ky_send.at[h if t is None else t],
            ky_recv.at[h if t is None else t],
            {"sect": other_y},
        )

    for i in range(1, halves):
        t = lax.rem(h + i, halves)
        copy = remote(
            kv_ref, kv_all.at[s], kz_send.at[t], kz_recv.at[h], {"sect": 2 * t + low}
        )
        copy.start()
        started.append(copy)
    copy = kv_cross(None)
    copy.start()
    started.append(copy)
    own_kv = pltpu.make_async_copy(kv_ref, kv_all.at[s], local_sem.at[0])
    own_kv.start()

    def w_piece(t):
        return w_ref.at[pl.ds(pl.multiple_of(t * w_rows + g * part, part), part), :]

    def w_place(group, t):
        span = pl.ds(pl.multiple_of(group * part, part), part)
        if len(w_out.shape) == 3:
            return w_out.at[t, span, :]
        return w_out.at[span, pl.ds(pl.multiple_of(t * w_cols, w_cols), w_cols)]

    for t in sect_peers:
        copy = remote(
            w_piece(t), w_place(g, s), w_send.at[t], w_recv.at[s], {"sect": t}
        )
        copy.start()
        started.append(copy)
    own_w = pltpu.make_async_copy(w_piece(s), w_place(g, s), local_sem.at[1])
    own_w.start()
    for i, t in enumerate(group_peers):
        copy = remote(
            w_piece(s), w_place(g, s), f_send.at[i, s], f_recv.at[g, s], {"groups": t}
        )
        copy.start()
        started.append(copy)

    for i in range(1, halves):
        t = lax.rem(h + i, halves)
        remote(
            kv_ref, kv_all.at[2 * t + low], kz_send.at[t], kz_recv.at[t], {"sect": 2 * t + low}
        ).wait_recv()
        copy = kv_cross(t)
        copy.start()
        started.append(copy)

    window = seg_k_ref.shape[1]
    first = jnp.maximum(s - (window // rows - 1), 0)
    q_pos = s * rows + lax.broadcasted_iota(jnp.int32, (rows, window), 0)
    k_pos = first * rows + lax.broadcasted_iota(jnp.int32, (rows, window), 1)
    allowed = jnp.logical_and(seg_q_ref[...] == seg_k_ref[...], k_pos <= q_pos)
    bias[...] = jnp.where(allowed, 0.0, MASKED)

    for i in range(halves):
        t = lax.rem(h + i, halves)
        remote(
            kv_ref, kv_all.at[2 * t + 1 - low], ky_send.at[t], ky_recv.at[t], {"sect": other_y}
        ).wait_recv()
    own_kv.wait()

    scale = 1.0 / math.sqrt(HEAD_WIDTH)
    kv_width = kv_heads * HEAD_WIDTH
    per_kv = q_ref.shape[1] // kv_heads

    def attend(i, carry):
        t = lax.rem(s + 1 + i, sects)
        kv_head = (t * cols) // per_kv
        k_col = pl.multiple_of(kv_head * HEAD_WIDTH, HEAD_WIDTH)
        v_col = pl.multiple_of(kv_width + kv_head * HEAD_WIDTH, HEAD_WIDTH)
        span = pl.ds(first, window // rows)
        keys = kv_all[span, :, pl.ds(k_col, HEAD_WIDTH)].reshape(window, HEAD_WIDTH)
        vals = kv_all[span, :, pl.ds(v_col, HEAD_WIDTH)].reshape(window, HEAD_WIDTH)
        for j in range(cols // HEAD_WIDTH):
            q_col = pl.multiple_of(t * cols + j * HEAD_WIDTH, HEAD_WIDTH)
            q = q_ref[:, pl.ds(q_col, HEAD_WIDTH)]
            scores = lax.dot_general(
                q, keys, (((1,), (1,)), ((), ())), preferred_element_type=jnp.float32
            )
            scores = scores * scale + bias[...]
            top = jnp.max(scores, axis=1, keepdims=True)
            weights = jnp.exp(scores - top).astype(jnp.bfloat16)
            total = jnp.sum(weights.astype(jnp.float32), axis=1, keepdims=True)
            mixed = jnp.dot(weights, vals, preferred_element_type=jnp.float32)
            att[t, :, j * HEAD_WIDTH : (j + 1) * HEAD_WIDTH] = (mixed / total).astype(
                jnp.bfloat16
            )
        return carry

    def a_place(t):
        return a_out.at[pl.ds(pl.multiple_of(t * rows, rows), rows), :]

    def a_copy(t):
        return remote(att.at[t], a_place(s), a_send.at[t], a_recv.at[s], {"sect": t})

    def step(i, carry):
        attend(i, carry)

        @pl.when(i >= 1)
        def _():
            a_copy(lax.rem(s + i, sects)).start()

        return carry

    lax.fori_loop(0, sects, step, 0)
    own_a = pltpu.make_async_copy(att.at[s], a_place(s), local_sem.at[2])
    own_a.start()

    for t in sect_peers:
        remote(
            w_piece(s), w_place(g, t), w_send.at[t], w_recv.at[t], {"sect": t}
        ).wait_recv()
        for i, u in enumerate(group_peers):
            copy = remote(
                w_place(g, t), w_place(g, t), f_send.at[i, t], f_recv.at[g, t], {"groups": u}
            )
            copy.start()
            started.append(copy)
    for t in sect_peers:
        remote(att.at[t], a_place(t), a_send.at[t], a_recv.at[t], {"sect": t}).wait_recv()
    for u in group_peers:
        for t in [s] + sect_peers:
            remote(
                w_place(g, t), w_place(u, t), f_send.at[0, t], f_recv.at[u, t], {"groups": u}
            ).wait_recv()
    own_w.wait()
    own_a.wait()
    for copy in started:
        copy.wait_send()
    for t in sect_peers:
        a_copy(t).wait_send()


def exchange_attention(queries, kv, seg_q, seg_k, proj_weight, kv_heads):
    groups = lax.axis_size("groups")
    sects = lax.axis_size("sect")
    rows, width = queries.shape
    cols = width // sects
    w_rows = proj_weight.shape[0] // sects
    w_cols = proj_weight.shape[1]
    aligned = w_cols % 128 == 0
    w_shape = (w_rows, w_cols * sects) if aligned else (sects, w_rows, w_cols)
    attended, weight = pl.pallas_call(
        functools.partial(attention_kernel, groups, sects, kv_heads),
        out_shape=(
            jax.ShapeDtypeStruct((rows * sects, cols), jnp.bfloat16),
            jax.ShapeDtypeStruct(w_shape, jnp.bfloat16),
        ),
        in_specs=[VMEM_SPEC, VMEM_SPEC, VMEM_SPEC, VMEM_SPEC, ANY_SPEC],
        out_specs=(ANY_SPEC, ANY_SPEC),
        scratch_shapes=[
            pltpu.VMEM((sects,) + kv.shape, jnp.bfloat16),
            pltpu.VMEM((sects, rows, cols), jnp.bfloat16),
            pltpu.VMEM((rows, seg_k.shape[1]), jnp.float32),
            DMA((sects // 2,)),
            DMA((sects // 2,)),
            DMA((sects // 2,)),
            DMA((sects // 2,)),
            DMA((sects,)),
            DMA((sects,)),
            DMA((sects,)),
            DMA((sects,)),
            DMA((groups, sects)),
            DMA((groups, sects)),
            DMA((3,)),
        ],
        compiler_params=pltpu.CompilerParams(collective_id=0, has_side_effects=True),
        name="attention",
    )(queries, kv, seg_q, seg_k, proj_weight)
    if not aligned:
        weight = weight.transpose(1, 0, 2).reshape(w_rows, w_cols * sects)
    return attended, weight


def positions():
    s = lax.axis_index("sect")
    c = lax.axis_index("head")
    halves = lax.axis_size("sect") // 2
    h = s // 2
    low = lax.rem(s, 2)
    partner = {"head": 1 - c}
    across = {"sect": 2 * h + 1 - low}
    others = [lax.rem(h + i, halves) for i in range(1, halves)]
    return s, c, h, low, halves, partner, across, others


def sum_kernel(
    p_ref, o_ref, rp, cs, ry, zs, rz, p_send, p_recv, y_send, y_recv, z_send, z_recv
):
    s, c, h, low, halves, partner, across, others = positions()
    greet([partner, across] + [{"sect": 2 * t + low} for t in others])
    order = others + [h]
    started = []

    def widen(x):
        return x.astype(jnp.float32)

    for t in order:
        copy = remote(
            p_ref.at[pl.ds(2 * t, 2), 1 - c], rp.at[t], p_send.at[t], p_recv.at[t], partner
        )
        copy.start()
        started.append(copy)
    for t in order:
        remote(
            p_ref.at[pl.ds(2 * t, 2), 1 - c], rp.at[t], p_send.at[t], p_recv.at[t], partner
        ).wait_recv()
        cs[t] = (widen(p_ref[2 * t + 1 - low, c]) + widen(rp[t, 1 - low])).astype(jnp.bfloat16)
        copy = remote(cs.at[t], ry.at[t], y_send.at[t], y_recv.at[t], across)
        copy.start()
        started.append(copy)
    for t in order:
        remote(cs.at[t], ry.at[t], y_send.at[t], y_recv.at[t], across).wait_recv()
        total = widen(p_ref[2 * t + low, c]) + widen(rp[t, low]) + widen(ry[t])
        if t is h:
            o_ref[...] = total
        else:
            zs[t] = total.astype(jnp.bfloat16)
            copy = remote(
                zs.at[t], rz.at[h], z_send.at[t], z_recv.at[h], {"sect": 2 * t + low}
            )
            copy.start()
            started.append(copy)
    for t in others:
        remote(
            zs.at[t], rz.at[t], z_send.at[t], z_recv.at[t], {"sect": 2 * t + low}
        ).wait_recv()
        o_ref[...] += widen(rz[t])
    for copy in started:
        copy.wait_send()


def sum_scatter(partial_rows, moe_rows, collective_id):
    sects = lax.axis_size("sect")
    heads = lax.axis_size("head")
    width = partial_rows.shape[1]
    halves = sects // 2
    block = (moe_rows, width)
    return pl.pallas_call(
        sum_kernel,
        out_shape=jax.ShapeDtypeStruct(block, jnp.float32),
        in_specs=[VMEM_SPEC],
        out_specs=VMEM_SPEC,
        scratch_shapes=[
            pltpu.VMEM((halves, 2) + block, jnp.bfloat16),
            pltpu.VMEM((halves,) + block, jnp.bfloat16),
            pltpu.VMEM((halves,) + block, jnp.bfloat16),
            pltpu.VMEM((halves,) + block, jnp.bfloat16),
            pltpu.VMEM((halves,) + block, jnp.bfloat16),
        ]
        + [DMA((halves,))] * 6,
        compiler_params=pltpu.CompilerParams(
            collective_id=collective_id, has_side_effects=True
        ),
        name="sum_scatter",
    )(partial_rows.reshape((sects, heads) + block))


def gather_kernel(
    x_ref, o_ref, p_send, p_recv, y_send, y_recv, z_send, z_recv, local_sem
):
    s, c, h, low, halves, partner, across, others = positions()
    greet([partner, across] + [{"sect": 2 * t + low} for t in others])
    started = []

    def send(src, row, send_sem, recv_sem, device):
        copy = remote(src, o_ref.at[row, c], send_sem, recv_sem, device)
        copy.start()
        started.append(copy)

    for t in others:
        send(x_ref, s, z_send.at[t], z_recv.at[h], {"sect": 2 * t + low})
    send(x_ref, s, y_send.at[h], y_recv.at[h], across)
    send(x_ref, s, p_send.at[s], p_recv.at[s], partner)
    own = pltpu.make_async_copy(x_ref, o_ref.at[s, c], local_sem)
    own.start()
    for t in others:
        row = 2 * t + low
        remote(x_ref, o_ref.at[row, c], z_send.at[t], z_recv.at[t], {"sect": row}).wait_recv()
        send(o_ref.at[row, c], row, y_send.at[t], y_recv.at[t], across)
        send(o_ref.at[row, c], row, p_send.at[row], p_recv.at[row], partner)
    for t in [h] + others:
        row = 2 * t + 1 - low
        remote(x_ref, o_ref.at[row, c], y_send.at[t], y_recv.at[t], across).wait_recv()
        send(o_ref.at[row, c], row, p_send.at[row], p_recv.at[row], partner)
    for t in [h] + others:
        for row in (2 * t + low, 2 * t + 1 - low):
            remote(
                x_ref, o_ref.at[row, 1 - c], p_send.at[row], p_recv.at[row], partner
            ).wait_recv()
    own.wait()
    for copy in started:
        copy.wait_send()


def gather_rows(x, collective_id):
    sects = lax.axis_size("sect")
    heads = lax.axis_size("head")
    halves = sects // 2
    out = pl.pallas_call(
        gather_kernel,
        out_shape=jax.ShapeDtypeStruct((sects, heads) + x.shape, x.dtype),
        in_specs=[VMEM_SPEC],
        out_specs=VMEM_SPEC,
        scratch_shapes=[
            DMA((sects,)),
            DMA((sects,)),
            DMA((halves,)),
            DMA((halves,)),
            DMA((halves,)),
            DMA((halves,)),
            DMA,
        ],
        compiler_params=pltpu.CompilerParams(
            collective_id=collective_id, has_side_effects=True
        ),
        name="gather_rows",
    )(x)
    return out.reshape(-1, x.shape[1])


def shards(
    queries,
    packed_key_rows,
    values,
    segments,
    proj_weight,
    residual,
    norm_gain,
    expert_ids,
    route_weights,
    gate_weight,
    up_weight,
    down_weight,
):
    rows = queries.shape[0]
    sects = lax.axis_size("sect")
    heads = lax.axis_size("head")
    s = lax.axis_index("sect")
    c = lax.axis_index("head")
    experts = sects * heads
    moe_rows, width = residual.shape
    kv_heads = packed_key_rows.shape[1] // HEAD_WIDTH

    blocks = min(sects, -(-segments.shape[0] // (2 * rows)) + 1)
    first = jnp.maximum(s - (blocks - 1), 0)
    seg_q = lax.dynamic_slice_in_dim(segments, s * rows, rows, 0)[:, None]
    seg_k = lax.dynamic_slice_in_dim(segments, first * rows, blocks * rows, 0)[None, :]
    kv = jnp.concatenate([packed_key_rows, values], axis=1)
    attended, weight = exchange_attention(queries, kv, seg_q, seg_k, proj_weight, kv_heads)
    partial_rows = jnp.dot(attended, weight, preferred_element_type=jnp.float32)
    projected = sum_scatter(partial_rows.astype(jnp.bfloat16), moe_rows, 1)

    hidden_mid = (residual.astype(jnp.float32) + projected).astype(jnp.bfloat16)
    mid_float = lax.optimization_barrier(hidden_mid).astype(jnp.float32)
    inverse = lax.rsqrt(jnp.mean(mid_float * mid_float, axis=1, keepdims=True) + NORM_EPS)
    normed = (mid_float * inverse * norm_gain.astype(jnp.float32)[None, :]).astype(jnp.bfloat16)

    route_share = route_weights / jnp.sum(route_weights, axis=1, keepdims=True)
    named = expert_ids[:, :, None] == jnp.arange(experts, dtype=jnp.int32)[None, None, :]
    share = jnp.sum(jnp.where(named, route_share[:, :, None], 0.0), axis=1)
    share_high = lax.reduce_precision(share, 8, 7)
    share_low = (share - share_high).astype(jnp.bfloat16)
    pad = -(2 * experts) % 128
    sent = jnp.concatenate(
        [
            normed,
            share_high.astype(jnp.bfloat16),
            share_low,
            jnp.zeros((moe_rows, pad), jnp.bfloat16),
        ],
        axis=1,
    )
    gathered = gather_rows(sent, 2)
    expert = s * heads + c
    all_rows = gathered[:, :width]
    pair = gathered[:, width:].astype(jnp.float32)
    lane = jnp.arange(pair.shape[1], dtype=jnp.int32)[None, :]
    mine = jnp.logical_or(lane == expert, lane == expert + experts)
    own_share = jnp.sum(jnp.where(mine, pair, 0.0), axis=1, keepdims=True)
    gate_act = jnp.dot(all_rows, gate_weight[0], preferred_element_type=jnp.float32)
    up_act = jnp.dot(all_rows, up_weight[0], preferred_element_type=jnp.float32)
    hidden = (jax.nn.silu(gate_act) * up_act).astype(jnp.bfloat16)
    result = jnp.dot(hidden, down_weight[0], preferred_element_type=jnp.float32)
    mixed = (result * own_share).astype(jnp.bfloat16)
    mixture = sum_scatter(mixed, moe_rows, 3)
    return (hidden_mid, mixture.astype(jnp.bfloat16))


def solution(mesh):
    rows = P(("groups", "sect", "head"), None)
    split = P(("groups", "sect"), "head")
    expert = P(("sect", "head"), None, None)
    placed = (
        split,
        split,
        split,
        P("groups"),
        P("head", "sect"),
        rows,
        P(),
        rows,
        rows,
        expert,
        expert,
        expert,
    )
    return jax.shard_map(
        shards, mesh=mesh, in_specs=placed, out_specs=(rows, rows), check_vma=False
    )
```

time: 463 us -> 247 us (0.53)
  waiting for transfers between devices: 205 us -> 0 us
  Pallas kernels: 0 us -> 202 us
  blocking collectives: 140 us -> 0 us
  local copies, waits for them, and re-layouts: 27.3 us -> 4.95 us
  matrix products: 46.1 us -> 26.8 us
  between operations: 15.5 us -> 0.73 us
  other arithmetic: 22.3 us -> 9.38 us
  starting transfers between devices: 5.76 us -> 0 us
    pallas_call x0 -> x4, Pallas kernels: none -> 202 us  [the longest x2 91.7 us: sum_scatter(): pl.pallas_call(sum_kernel, out_shape=jax.ShapeDtypeStruct(block, jnp.floa...]
    all_gather x1 -> x0, waiting for transfers between devices: 128 us -> none  [shards(): lax.all_gather(proj_weight, 'sect', axis=1, tiled=True)]
    all_to_all x1 -> x0, blocking collectives: 75.4 us -> none  [shards(): lax.all_to_all(parcels, ('sect', 'head'), split_axis=0, concat_axis=0, ti...]
    all_to_all x1 -> x0, waiting for transfers between devices: 69.5 us -> none  [shards(): lax.all_to_all(processed, ('sect', 'head'), split_axis=0, concat_axis=0,...]
    all_gather x2 -> x0, blocking collectives: 64.4 us -> none  [the longest x1 33 us: attend(): value_piece = lax.all_gather(values, 'sect', axis=0, tiled=True)]
    dot_general x5 -> x3, matrix products: 46.1 us -> 26.8 us  [the longest x1 12.3 us: shards(): result = jnp.dot(hidden, down_weight[0], preferred_element_type=jnp.float32)]
    reduce_sum x5 -> x3, other arithmetic: 14.5 us -> 1.95 us  [the longest x1 1.09 us: shards(): own_share = jnp.sum(jnp.where(mine, pair, 0.0), axis=1, keepdims=True)]
    gather x2 -> x0, local copies, waits for them, and re-layouts: 9.35 us -> none  [the longest x1 7.58 us: shards(): gathered = returned_flat[slot_index].reshape(moe_rows, top_count, -1)]
  transfers between devices with their start and end apart: 3 -> 0, of which waited for: 3 -> 0; matrix products, arithmetic and copies ran while one was open for 11% -> 0% of each run, Pallas kernels for 0% -> 0%
where the time goes in v1:
time: 247 us; the launch traced here: 244 us
  Pallas kernels  202 us (82%)
  matrix products  26.8 us (11%)
  other arithmetic  9.38 us (4%)
  local copies, waits for them, and re-layouts  4.95 us (2%)
    pallas_call x2, Pallas kernels, sum_scatter(): pl.pallas_call(sum_kernel, out_shape=jax.ShapeDtypeStruct(block, jnp.floa...  91.7 us
    pallas_call x1, Pallas kernels, exchange_attention(): pl.pallas_call(functools.partial(attention_kernel, groups, sects, kv_head...  61 us
    pallas_call x1, Pallas kernels, gather_rows(): pl.pallas_call(gather_kernel, out_shape=jax.ShapeDtypeStruct((sects, head...  49.4 us
    dot_general x1, matrix products, shards(): result = jnp.dot(hidden, down_weight[0], preferred_element_type=jnp.float32)  12.3 us
    dot_general x1, matrix products, shards(): jnp.dot(all_rows, gate_weight[0], preferred_element_type=jnp.float32)  8.29 us
    dot_general x1, matrix products, shards(): partial_rows = jnp.dot(attended, weight, preferred_element_type=jnp.float32)  6.19 us

profile of v1, /device:TPU:17, one launch (start us, length us, event | category | flops | bytes accessed | tf_op | source)
XLA Modules:
  0.0 243.9 jit_solution(506469354832297117)
XLA Ops:
  0.7 0.9 dynamic-slice_bitcast_fusion
  1.6 0.7 reduce_sum.37
  2.3 0.7 broadcast_divide_fusion
  3.0 0.8 dynamic_slice.7
  3.8 0.6 broadcast_in_dim.42.seg_k_ref
  4.4 0.7 select_reduce_fusion.1
  5.1 0.7 convert_element_type.40
  5.8 0.1 copy.22
  5.8 0.1 copy.21
  5.9 0.7 copy.20.seg_q_ref
  6.7 1.5 pad_maximum_fusion.kv_ref
  8.2 61.0 %attention.1 = (bf16[1024,512]{1,0:T(8,128)(2,1)}, bf16[512,2048]{1,0:T(8,128)(2,1)}) custom-call(bf16[128,4096]{1,0:T(8,128)(2,1)} %q_ref.1, bf16[128,512]{1,0:T(8,128)(2,1)} %pad_maximum_fusion.kv_ref, s32[128,1]{1,0:T(8,128)} %copy.20.seg_q_ref, s32[1,640]{1,0:T(1,128)} %broadcast_in_dim.42.seg_k_ref, bf16[4096,256]{1,0:T(8,128)(2,1)} %w_ref.1), custom_call_target="tpu_custom_call" | custom-call | tf_op jit(solution)/shard_map/attention/pallas_call | solution.py:230
  69.3 6.2 %convolution_convert_fusion = bf16[1024,2048]{1,0:T(8,128)(2,1)} fusion(bf16[1024,512]{1,0:T(8,128)(2,1)} %get-tuple-element.4, bf16[512,2048]{1,0:T(8,128)(2,1)} %get-tuple-element.5), kind=kOutput, calls=%fused_computation.1 | convolution fusion | flops 2149580800 | bytes 7340032 | tf_op jit(solution)/shard_map/dot_general | solution.py:438
  75.5 49.2 %sum_scatter.2 = f32[64,2048]{1,0:T(8,128)} custom-call(bf16[8,2,64,2048]{3,2,1,0:T(8,128)(2,1)} %bitcast.24), custom_call_target="tpu_custom_call" | custom-call | tf_op jit(solution)/shard_map/sum_scatter/pallas_call | solution.py:326
  124.6 1.2 add_convert_fusion
  125.8 0.2 fusion.15
  126.0 0.8 fusion.17
  126.8 1.7 concatenate.7.x_ref
  128.5 49.4 %gather_rows.1 = bf16[8,2,64,2176]{3,2,1,0:T(8,128)(2,1)} custom-call(bf16[64,2176]{1,0:T(8,128)(2,1)} %concatenate.7.x_ref), custom_call_target="tpu_custom_call" | custom-call | tf_op jit(solution)/shard_map/gather_rows/pallas_call | solution.py:387
  177.9 1.1 select_reduce_fusion
  179.0 8.3 %fusion.2 = f32[1024,768]{1,0:T(8,128)} fusion(bf16[1024,2176]{1,0:T(8,128)(2,1)} %bitcast.21, bf16[1,2048,768]{2,1,0:T(8,128)(2,1)} %param.21), kind=kOutput, calls=%fused_computation.4 | convolution fusion | flops 3221225472 | bytes 10485760 | tf_op jit(solution)/shard_map/dot_general | solution.py:468
  187.3 12.3 %multiply_convert_fusion = bf16[1024,2048]{1,0:T(8,128)(2,1)} fusion(f32[1024]{0:T(1024)S(1)} %select_reduce_fusion, bf16[1,768,2048]{2,1,0:T(8,128)(2,1)S(1)} %copy-done, f32[1024,768]{1,0:T(8,128)} %fusion.2, bf16[1,2048,768]{2,1,0:T(8,128)(2,1)} %param.22, bf16[1024,2176]{1,0:T(8,128)(2,1)} %bitcast.22), kind=kOutput, calls=%fused_computation | convolution fusion | flops 6451363840 | bytes 17829888 | tf_op jit(solution)/shard_map/dot_general | solution.py:471
  199.6 42.5 %sum_scatter.3 = f32[64,2048]{1,0:T(8,128)} custom-call(bf16[8,2,64,2048]{3,2,1,0:T(8,128)(2,1)} %bitcast.23), custom_call_target="tpu_custom_call" | custom-call | tf_op jit(solution)/shard_map/sum_scatter/pallas_call | solution.py:326
  242.1 1.8 convert_element_type.47
  (9 shorter events, 0.0 us)
Async XLA Ops:
  0.6 186.7 %copy-start = (bf16[1,768,2048]{2,1,0:T(8,128)(2,1)S(1)}, bf16[1,768,2048]{2,1,0:T(8,128)(2,1)}, u32[]{:S(2)}) copy-start(bf16[1,768,2048]{2,1,0:T(8,128)(2,1)} %param.23) | copy-start | bytes 9437188
  125.8 53.3 %copy-start.1 = (bf16[64,2048]{1,0:T(8,128)(2,1)}, bf16[64,2048]{1,0:T(8,128)(2,1)S(1)}, u32[]{:S(2)}) copy-start(bf16[64,2048]{1,0:T(8,128)(2,1)S(1)} %add_convert_fusion) | copy-start | bytes 786436
